TPU v7x, 512 devices: a whole 4x8x8 slice. The times are simulated.
512 devices in a mesh: region: 32 (over y, x_lo, core), grp: 16 (over z, x_hi).
Axes of the slice: x: 4 (x_hi: 2, x_lo: 2; x = x_hi * 2 + x_lo), y: 8, z: 8, core: 2. Of those that a mesh axis runs over, the one named last changes fastest.
Arguments:
- transmission: float32 [2, 640, 20480], P(None, 'grp', 'region'), may hold values from -3 to 3
- probe: bfloat16 [2, 8, 512, 512], P(None, None, 'grp'), may hold values from -1.5 to 1.5
- measured: float32 [32, 512, 512], P('region', 'grp'), may hold values from 0 to 2
- positions: int32 [32, 2], P('region'), may hold values from 0 to 128
- past_steps: float32 [4, 2, 640, 20480], P(None, None, 'grp', 'region'), may hold values from -40 to 40
- past_changes: float32 [3, 2, 640, 20480], P(None, None, 'grp', 'region'), may hold values from -240 to 240
- old_gradient: float32 [2, 640, 20480], P(None, 'grp', 'region'), may hold values from -40 to 40
Outputs:
- updated: float32 [2, 640, 20480], P(None, 'grp', 'region')
- gradient: float32 [2, 640, 20480], P(None, 'grp', 'region')
All inputs are finite; a program needn't handle non-finite values.
Results may differ from a plain program's by a relative error of at most 0.019.
The roundings to bfloat16 on the way count: a program that leaves them out, or rounds other values in their place, can miss the bound.
Values may be sent and summed in bfloat16 or wider, within the bound.
A program may use at most 64 MiB of HBM per device.

v0:
```python
import math
import jax
import jax.numpy as jnp
from jax import lax
from jax.sharding import PartitionSpec as P

TWO_PI = 2.0 * math.pi
CURVE_FLOOR = 0.25
TIKHONOV = 0.5
EPSILON = 1e-06


def dft_tables(count):
    index = jnp.arange(count, dtype=jnp.int32)
    phase = (index[:, None] * index[None, :] % count).astype(jnp.float32) * (TWO_PI / count)
    factor = 1.0 / math.sqrt(count)
    return (
        (jnp.cos(phase) * factor).astype(jnp.bfloat16),
        (-jnp.sin(phase) * factor).astype(jnp.bfloat16),
    )


def chirp_table(count):
    index = jnp.arange(count, dtype=jnp.int32)
    wavenumber = (index + count // 2) % count - count // 2
    phase = (wavenumber * wavenumber % (4 * count)).astype(jnp.float32) * (TWO_PI / (4 * count))
    return (jnp.cos(phase), -jnp.sin(phase))


def rotate(real_part, imag_part, turn_real, turn_imag):
    return (
        real_part * turn_real - imag_part * turn_imag,
        real_part * turn_imag + imag_part * turn_real,
    )


def narrow(pair):
    return jnp.stack([pair[0], pair[1]]).astype(jnp.bfloat16)


def right_product(field, matrix_real, matrix_imag):

    def single(left, right):
        return jnp.einsum("...k,kj->...j", left, right, preferred_element_type=jnp.float32)

    return (
        single(field[0], matrix_real) - single(field[1], matrix_imag),
        single(field[0], matrix_imag) + single(field[1], matrix_real),
    )


def left_product(matrix_real, matrix_imag, field):

    def single(left, right):
        return jnp.einsum("jk,...kc->...jc", left, right, preferred_element_type=jnp.float32)

    return (
        single(matrix_real, field[0]) - single(matrix_imag, field[1]),
        single(matrix_real, field[1]) + single(matrix_imag, field[0]),
    )


def shards(transmission, probe, measured, positions, past_steps, past_changes, old_gradient):
    member = lax.axis_index("grp")
    frame_len = probe.shape[3]
    rows_here = probe.shape[2]
    tile_len = transmission.shape[2]
    anchor = jnp.zeros((), jnp.int32)
    fwd_real, fwd_imag = dft_tables(frame_len)
    inv_imag = -fwd_imag
    chirp_real, chirp_imag = chirp_table(frame_len)
    probe_wide = probe.astype(jnp.float32)
    tile = lax.all_gather(transmission.astype(jnp.bfloat16), "grp", axis=1, tiled=True)
    frame = 0
    first_row = positions[frame, 0] + member * rows_here
    window = jnp.swapaxes(
        lax.dynamic_slice(
            tile, (anchor, positions[frame, 1], first_row), (2, frame_len, rows_here)
        ),
        1,
        2,
    ).astype(jnp.float32)
    wave = narrow(rotate(probe_wide[0], probe_wide[1], window[0], window[1]))
    section = narrow(rotate(*right_product(wave, fwd_real, fwd_imag), chirp_real, chirp_imag))
    spread = narrow(right_product(section, fwd_real, inv_imag))
    section = narrow(
        rotate(
            *left_product(
                fwd_real,
                fwd_imag,
                lax.all_to_all(spread, "grp", split_axis=3, concat_axis=2, tiled=True),
            ),
            chirp_real[:, None],
            chirp_imag[:, None]
        )
    )
    far_field = narrow(left_product(fwd_real, inv_imag, section))
    near_rows = lax.all_to_all(far_field, "grp", split_axis=2, concat_axis=3, tiled=True)
    field_wide = near_rows.astype(jnp.float32)
    misfit = (
        jnp.sum(field_wide[0] * field_wide[0] + field_wide[1] * field_wide[1], axis=0)
        - measured[frame]
    )
    weighted = (misfit * field_wide).astype(jnp.bfloat16)
    section = narrow(
        rotate(
            *left_product(
                fwd_real,
                fwd_imag,
                lax.all_to_all(weighted, "grp", split_axis=3, concat_axis=2, tiled=True),
            ),
            chirp_real[:, None],
            -chirp_imag[:, None]
        )
    )
    returned = narrow(left_product(fwd_real, inv_imag, section))
    section = narrow(
        rotate(
            *right_product(
                lax.all_to_all(returned, "grp", split_axis=2, concat_axis=3, tiled=True),
                fwd_real,
                fwd_imag,
            ),
            chirp_real,
            -chirp_imag
        )
    )
    back_wave = jnp.stack(right_product(section, fwd_real, inv_imag))
    grad_real = 4.0 * jnp.sum(probe_wide[0] * back_wave[0] + probe_wide[1] * back_wave[1], axis=0)
    grad_imag = 4.0 * jnp.sum(probe_wide[0] * back_wave[1] - probe_wide[1] * back_wave[0], axis=0)
    frame_grads = [jnp.stack([grad_real, grad_imag])]
    scattered = jnp.zeros((2, tile_len, tile_len), jnp.float32)
    frame = 0
    corner = (anchor, positions[frame, 1], positions[frame, 0] + member * rows_here)
    scattered = lax.dynamic_update_slice(scattered, jnp.swapaxes(frame_grads[frame], 1, 2), corner)
    data_grad = lax.psum_scatter(
        scattered.astype(jnp.bfloat16), "grp", scatter_dimension=1, tiled=True
    ).astype(jnp.float32)
    gradient = data_grad + TIKHONOV * transmission
    depth = past_steps.shape[0]
    last = depth - 1
    change_new = gradient - old_gradient
    steps_list = [past_steps[index] for index in range(depth)]
    changes = [past_changes[index] for index in range(depth - 1)] + [change_new]
    alphas = [None] * depth
    curvature, self_dots, change_norm = lax.psum(
        (
            jnp.stack([jnp.sum(steps_list[index] * changes[index]) for index in range(depth)]),
            jnp.sum(past_steps * past_steps, axis=(1, 2, 3)),
            jnp.sum(change_new * change_new),
        ),
        ("region", "grp"),
    )
    weights = [
        1.0 / jnp.maximum(curvature[index], CURVE_FLOOR * self_dots[index])
        for index in range(depth)
    ]
    direction = gradient
    for index in reversed(range(depth)):
        alphas[index] = weights[index] * lax.psum(
            jnp.sum(steps_list[index] * direction), ("region", "grp")
        )
        direction = direction - alphas[index] * changes[index]
    scale = jnp.maximum(curvature[last], CURVE_FLOOR * self_dots[last]) / (change_norm + EPSILON)
    direction = scale * direction
    for index in range(depth):
        beta = weights[index] * lax.psum(jnp.sum(changes[index] * direction), ("region", "grp"))
        direction = direction + (alphas[index] - beta) * steps_list[index]
    return (transmission - direction, gradient)


def solution(mesh):
    return jax.shard_map(
        shards,
        mesh=mesh,
        in_specs=(
            P(None, "grp", "region"),
            P(None, None, "grp", None),
            P("region", "grp", None),
            P("region", None),
            P(None, None, "grp", "region"),
            P(None, None, "grp", "region"),
            P(None, "grp", "region"),
        ),
        out_specs=(P(None, "grp", "region"), P(None, "grp", "region")),
        check_vma=False,
    )
```

profile of v0, /device:TPU:27, one launch (start us, length us, event | category | flops | bytes accessed | tf_op | source)
XLA Modules:
  0.0 1377.4 jit_solution(13313109563345839940)
XLA Ops:
  13.6 86.9 %all-gather.2.cloned.1.call-done = bf16[2,640,640]{2,1,0:T(8,128)(2,1)} async-done(((bf16[2,40,640]{2,1,0:T(8,128)(2,1)}), bf16[2,640,640]{2,1,0:T(8,128)(2,1)}) %all-gather.2.cloned.1.call-update) | async-done | bytes 1638416 | tf_op jit(solution)/shard_map/all_gather | solution.py:73
  102.2 4.4 fusion.71
  106.7 4.5 fusion.42
  111.1 4.5 convolution_subtract_fusion.7
  115.6 4.8 add_convert_fusion.3
  120.4 4.4 fusion.68
  124.8 4.5 fusion.32
  129.3 5.0 fusion.13
  134.3 4.7 fusion.12
  145.5 19.9 %all_to_all.54 = bf16[16,2,8192]{2,1,0:T(2,128)(2,1)} all-to-all(bf16[16,2,8192]{2,1,0:T(2,128)(2,1)} %reshape.161), channel_id=1, replica_groups=mesh['region'=32,'grp'=16] {'grp'}, dimensions={0} | all-to-all | bytes 1048576 | tf_op jit(solution)/shard_map/all_to_all | solution.py:91
  171.2 5.3 fusion.63
  177.5 4.4 fusion.65
  182.0 4.5 convolution_add_fusion.5
  186.5 4.8 fusion.84
  191.3 15.0 %fusion.61 = f32[8,32,512]{2,1,0:T(8,128)S(1)} fusion(bf16[8,512,32]{1,2,0:T(8,128)(2,1)S(1)} %get-tuple-element.35), kind=kOutput, calls=%fused_computation.97 | convolution fusion | flops 138412032 | bytes 786432 | tf_op jit(solution)/shard_map/jk,...kc->...jc/dot_general | solution.py:55
  206.3 4.4 fusion.59
  210.7 4.7 fusion.11
  215.4 4.7 fusion.10
  226.6 18.4 %all_to_all.55 = bf16[16,2,8192]{2,1,0:T(2,128)(2,1)} all-to-all(bf16[16,2,8192]{2,1,0:T(2,128)(2,1)} %reshape.163), channel_id=1, replica_groups=mesh['region'=32,'grp'=16] {'grp'}, dimensions={0} | all-to-all | bytes 1048576 | tf_op jit(solution)/shard_map/all_to_all | solution.py:98
  264.0 4.6 all-to-all-start.2
  268.8 13.5 all-to-all-done.2
  295.3 5.3 fusion.55
  303.1 4.4 fusion.57
  307.6 4.5 convolution_add_fusion.3
  312.1 5.2 fusion.86
  317.3 4.4 fusion.53
  321.7 4.4 fusion.51
  326.1 4.7 fusion.9
  330.9 4.7 fusion.8
  342.0 17.8 %all_to_all.56 = bf16[16,2,8192]{2,1,0:T(2,128)(2,1)} all-to-all(bf16[16,2,8192]{2,1,0:T(2,128)(2,1)} %reshape.167), channel_id=1, replica_groups=mesh['region'=32,'grp'=16] {'grp'}, dimensions={0} | all-to-all | bytes 1048576 | tf_op jit(solution)/shard_map/all_to_all | solution.py:120
  365.5 4.4 fusion.49
  370.0 5.4 fusion.35
  376.4 4.5 convolution_subtract_fusion.1
  380.9 4.8 add_convert_fusion
  385.7 4.6 fusion.46
  390.3 4.5 fusion.25
  394.8 4.5 convolution_subtract_fusion
  399.3 4.8 fusion.22
  404.4 4.4 dynamic_update_slice.3
  412.2 163.5 %reduce-scatter.4.cloned.1.call-done = bf16[40,1280]{1,0:T(8,128)(2,1)} async-done(((bf16[640,1280]{1,0:T(8,128)(2,1)}), bf16[40,1280]{1,0:T(8,128)(2,1)}) %reduce-scatter.4.cloned.1.call-update) | async-done | bytes 102416
  580.0 102.1 %all-reduce.1 = (f32[4]{0:T(128)S(1)}, f32[4]{0:T(128)S(1)}, f32[]{:T(128)}) all-reduce(f32[4]{0:T(128)S(1)} %pad_maximum_fusion.4, f32[4]{0:T(128)S(1)} %multiply_reduce_fusion, f32[]{:T(128)} %get-tuple-element.7), channel_id=1, replica_groups=mesh['region'=32,'grp'=16] {'region','grp'}, use_global_device_ids=true, to_apply=%region_8.9 | all-reduce | flops 9 | bytes 72 | tf_op jit(solution)/shard_map/psum | solution.py:146
  685.9 95.6 %psum.81 = f32[]{:T(128)} all-reduce(f32[]{:T(128)} %fusion.95), channel_id=1, replica_groups=mesh['region'=32,'grp'=16] {'region','grp'}, use_global_device_ids=true, to_apply=%region_16.17 | all-reduce | flops 1 | bytes 8 | tf_op jit(solution)/shard_map/psum | solution.py:160
  784.1 95.9 %psum.82 = f32[]{:T(128)} all-reduce(f32[]{:T(128)} %get-tuple-element.19), channel_id=1, replica_groups=mesh['region'=32,'grp'=16] {'region','grp'}, use_global_device_ids=true, to_apply=%region_18.19 | all-reduce | flops 1 | bytes 8 | tf_op jit(solution)/shard_map/psum | solution.py:160
  882.6 95.7 %all-reduce = (f32[]{:T(128)}, f32[]{:T(128)}) all-reduce(f32[]{:T(128)} %fusion.106, f32[]{:T(128)} %get-tuple-element.9), channel_id=1, replica_groups=mesh['region'=32,'grp'=16] {'region','grp'}, use_global_device_ids=true, to_apply=%region_20.21 | all-reduce | flops 2 | bytes 16 | tf_op jit(solution)/shard_map/psum | solution.py:160
  981.5 95.9 %psum.84 = f32[]{:T(128)} all-reduce(f32[]{:T(128)} %get-tuple-element.17), channel_id=1, replica_groups=mesh['region'=32,'grp'=16] {'region','grp'}, use_global_device_ids=true, to_apply=%region_22.23 | all-reduce | flops 1 | bytes 8 | tf_op jit(solution)/shard_map/psum | solution.py:167
  1078.8 95.7 %psum.85 = f32[]{:T(128)} all-reduce(f32[]{:T(128)} %fusion.99), channel_id=1, replica_groups=mesh['region'=32,'grp'=16] {'region','grp'}, use_global_device_ids=true, to_apply=%region_24.25 | all-reduce | flops 1 | bytes 8 | tf_op jit(solution)/shard_map/psum | solution.py:167
  1175.9 95.8 %psum.86 = f32[]{:T(128)} all-reduce(f32[]{:T(128)} %get-tuple-element.15), channel_id=1, replica_groups=mesh['region'=32,'grp'=16] {'region','grp'}, use_global_device_ids=true, to_apply=%region_26.27 | all-reduce | flops 1 | bytes 8 | tf_op jit(solution)/shard_map/psum | solution.py:167
  1273.1 95.7 %psum.87 = f32[]{:T(128)} all-reduce(f32[]{:T(128)} %multiply_reduce_fusion.1), channel_id=1, replica_groups=mesh['region'=32,'grp'=16] {'region','grp'}, use_global_device_ids=true, to_apply=%region_28.29 | all-reduce | flops 1 | bytes 8 | tf_op jit(solution)/shard_map/psum | solution.py:167
  (88 shorter events, 87.9 us)
Async XLA Ops:
  7.2 93.4 %all-gather.2.cloned.1.call-start = ((), (), s32[]{:S(2)}) async-start(), calls=%async_computation.5 | async-start | bytes 1740800 | tf_op jit(solution)/shard_map/all_gather | solution.py:73
  177.5 4.4 copy-start.7
  254.7 2.8 copy-start.5
  264.0 18.2 %all-to-all-start.2 = ((bf16[16,2,8192]{2,1,0:T(2,128)(2,1)}), bf16[16,2,8192]{2,1,0:T(2,128)(2,1)}, u32[]{:S(2)}, u32[]{:S(2)}) async-start(bf16[16,2,8192]{2,1,0:T(2,128)(2,1)} %reshape.165), calls=%async_computation.2 | async-start | bytes 1048576 | tf_op jit(solution)/shard_map/all_to_all | solution.py:110
  268.7 307.0 %reduce-scatter.4.cloned.1.call-start = ((), (), s32[]{:S(2)}) async-start(), calls=%async_computation.6 | async-start | bytes 1740800
  303.1 4.4 copy-start.6
  376.4 4.5 copy-start.8
  410.5 1.5 copy-start
  412.0 164.7 %copy-start.1 = (f32[3,2,40,640]{3,2,1,0:T(8,128)S(1)}, f32[3,2,40,640]{3,2,1,0:T(8,128)}, u32[]{:S(2)}) copy-start(f32[3,2,40,640]{3,2,1,0:T(8,128)} %param.12) | copy-start | bytes 1843204
  412.0 164.7 %copy-start.2 = (f32[2,40,640]{2,1,0:T(8,128)S(1)}, f32[2,40,640]{2,1,0:T(8,128)}, u32[]{:S(2)}) copy-start(f32[2,40,640]{2,1,0:T(8,128)} %param.7) | copy-start | bytes 614404
  412.0 164.7 %copy-start.4 = (f32[2,40,640]{2,1,0:T(8,128)S(1)}, f32[2,40,640]{2,1,0:T(8,128)}, u32[]{:S(2)}) copy-start(f32[2,40,640]{2,1,0:T(8,128)} %param.13) | copy-start | bytes 614404
  577.5 598.4 %copy-start.3 = (f32[2,40,640]{2,1,0:T(8,128)}, f32[2,40,640]{2,1,0:T(8,128)S(1)}, u32[]{:S(2)}) copy-start(f32[2,40,640]{2,1,0:T(8,128)S(1)} %get-tuple-element.22) | copy-start | bytes 614404
Sparse Core Ops, SparseCore 0:
  11.8 88.7 all-gather.1
  412.1 163.5 reduce-scatter.3
where the time goes:
time: 1390 us; the launch traced here: 1380 us
  blocking collectives  828 us (60%)
  waiting for transfers between devices  264 us (19%)
  matrix products  160 us (12%)
  local copies, waits for them, and re-layouts  72.7 us (5%)
  between operations  28.3 us (2%)
  other arithmetic  19.4 us (1%)
    psum x4, blocking collectives, shards(): lax.psum(jnp.sum(changes[index] * direction), ('region', 'grp'))  383 us
    psum x3, blocking collectives, shards(): lax.psum(jnp.sum(steps_list[index] * direction), ('region', 'grp'))  287 us
    unnamed x3, waiting for transfers between devices  164 us
    psum x1, blocking collectives, shards(): lax.psum((jnp.stack([jnp.sum(steps_list[index] * changes[index]) for inde...  102 us
    all_gather x1, waiting for transfers between devices, shards(): lax.all_gather(transmission.astype(jnp.bfloat16), 'grp', axis=1, tiled=True)  86.9 us
    dot_general x16, matrix products, single(): jnp.einsum('jk,...kc->...jc', left, right, preferred_element_type=jnp.flo...  85.7 us
    dot_general x16, matrix products, single(): jnp.einsum('...k,kj->...j', left, right, preferred_element_type=jnp.float32)  74.2 us
  transfers between devices with their start and end apart: 3, of which 3 were waited for; matrix products, arithmetic and copies ran while one was open for 0% of the time, Pallas kernels for 0%

commit v1 on v0

--- a/solution.py
+++ b/solution.py
@@ -144,12 +144,15 @@
     changes = [past_changes[index] for index in range(depth - 1)] + [change_new]
     alphas = [None] * depth
     curvature, self_dots, change_norm = lax.psum(
-        (
-            jnp.stack([jnp.sum(steps_list[index] * changes[index]) for index in range(depth)]),
-            jnp.sum(past_steps * past_steps, axis=(1, 2, 3)),
-            jnp.sum(change_new * change_new),
+        lax.psum(
+            (
+                jnp.stack([jnp.sum(steps_list[index] * changes[index]) for index in range(depth)]),
+                jnp.sum(past_steps * past_steps, axis=(1, 2, 3)),
+                jnp.sum(change_new * change_new),
+            ),
+            "grp",
         ),
-        ("region", "grp"),
+        "region",
     )
     weights = [
         1.0 / jnp.maximum(curvature[index], CURVE_FLOOR * self_dots[index])

time: 1390 us -> 1480 us (1.065)
  the two profiles are of different devices: /device:TPU:27 before, /device:TPU:25 now
where the time goes in v1:
time: 1480 us; the launch traced here: 1470 us
  blocking collectives  920 us (62%)
  waiting for transfers between devices  266 us (18%)
  matrix products  160 us (11%)
  local copies, waits for them, and re-layouts  72.9 us (5%)
  between operations  28.4 us (2%)
  other arithmetic  19.6 us (1%)
    psum x4, blocking collectives, shards(): lax.psum(jnp.sum(steps_list[index] * direction), ('region', 'grp'))  388 us
    psum x4, blocking collectives, shards(): lax.psum(jnp.sum(changes[index] * direction), ('region', 'grp'))  383 us
    unnamed x3, waiting for transfers between devices  165 us
    all_gather x1, waiting for transfers between devices, shards(): lax.all_gather(transmission.astype(jnp.bfloat16), 'grp', axis=1, tiled=True)  87.8 us
    dot_general x16, matrix products, single(): jnp.einsum('jk,...kc->...jc', left, right, preferred_element_type=jnp.flo...  85.7 us
    dot_general x16, matrix products, single(): jnp.einsum('...k,kj->...j', left, right, preferred_element_type=jnp.float32)  74.2 us
    psum x1, blocking collectives, shards(): lax.psum(lax.psum((jnp.stack([jnp.sum(steps_list[index] * changes[index])...  61.2 us
    psum x1, blocking collectives, shards(): lax.psum((jnp.stack([jnp.sum(steps_list[index] * changes[index]) for inde...  32.8 us
  transfers between devices with their start and end apart: 3, of which 3 were waited for; matrix products, arithmetic and copies ran while one was open for 0% of the time, Pallas kernels for 0%

profile of v1, /device:TPU:25, one launch (start us, length us, event | category | flops | bytes accessed | tf_op | source)
XLA Modules:
  0.0 1471.4 jit_solution(1240624283027758445)
XLA Ops:
  13.6 87.8 %all-gather.2.cloned.1.call-done = bf16[2,640,640]{2,1,0:T(8,128)(2,1)} async-done(((bf16[2,40,640]{2,1,0:T(8,128)(2,1)}), bf16[2,640,640]{2,1,0:T(8,128)(2,1)}) %all-gather.2.cloned.1.call-update) | async-done | bytes 1638416 | tf_op jit(solution)/shard_map/all_gather | solution.py:73
  103.2 4.4 fusion.71
  107.6 4.5 fusion.42
  112.1 4.5 convolution_subtract_fusion.7
  116.6 4.8 add_convert_fusion.3
  121.3 4.4 fusion.68
  125.8 4.5 fusion.32
  130.2 5.0 fusion.13
  135.3 4.7 fusion.12
  146.4 18.9 %all_to_all.54 = bf16[16,2,8192]{2,1,0:T(2,128)(2,1)} all-to-all(bf16[16,2,8192]{2,1,0:T(2,128)(2,1)} %reshape.161), channel_id=1, replica_groups=mesh['region'=32,'grp'=16] {'grp'}, dimensions={0} | all-to-all | bytes 1048576 | tf_op jit(solution)/shard_map/all_to_all | solution.py:91
  171.0 5.3 fusion.63
  177.4 4.4 fusion.65
  181.8 4.5 convolution_add_fusion.5
  186.3 4.8 fusion.84
  191.1 15.0 %fusion.61 = f32[8,32,512]{2,1,0:T(8,128)S(1)} fusion(bf16[8,512,32]{1,2,0:T(8,128)(2,1)S(1)} %get-tuple-element.36), kind=kOutput, calls=%fused_computation.97 | convolution fusion | flops 138412032 | bytes 786432 | tf_op jit(solution)/shard_map/jk,...kc->...jc/dot_general | solution.py:55
  206.1 4.4 fusion.59
  210.6 4.7 fusion.11
  215.3 4.7 fusion.10
  226.4 18.5 %all_to_all.55 = bf16[16,2,8192]{2,1,0:T(2,128)(2,1)} all-to-all(bf16[16,2,8192]{2,1,0:T(2,128)(2,1)} %reshape.163), channel_id=1, replica_groups=mesh['region'=32,'grp'=16] {'grp'}, dimensions={0} | all-to-all | bytes 1048576 | tf_op jit(solution)/shard_map/all_to_all | solution.py:98
  268.4 13.4 all-to-all-done.2
  294.9 5.3 fusion.55
  307.2 4.5 convolution_add_fusion.3
  311.7 5.2 fusion.86
  316.9 4.4 fusion.53
  321.3 4.4 fusion.51
  325.8 4.7 fusion.9
  330.5 4.7 fusion.8
  341.6 17.8 %all_to_all.56 = bf16[16,2,8192]{2,1,0:T(2,128)(2,1)} all-to-all(bf16[16,2,8192]{2,1,0:T(2,128)(2,1)} %reshape.167), channel_id=1, replica_groups=mesh['region'=32,'grp'=16] {'grp'}, dimensions={0} | all-to-all | bytes 1048576 | tf_op jit(solution)/shard_map/all_to_all | solution.py:120
  365.2 4.4 fusion.49
  369.6 5.4 fusion.35
  376.0 4.5 convolution_subtract_fusion.1
  380.5 4.8 add_convert_fusion
  385.3 4.6 fusion.46
  389.9 4.5 fusion.25
  394.4 4.5 convolution_subtract_fusion
  398.9 4.8 fusion.22
  404.0 4.5 dynamic_update_slice.3
  412.0 164.6 %reduce-scatter.4.cloned.1.call-done = bf16[40,1280]{1,0:T(8,128)(2,1)} async-done(((bf16[640,1280]{1,0:T(8,128)(2,1)}), bf16[40,1280]{1,0:T(8,128)(2,1)}) %reduce-scatter.4.cloned.1.call-update) | async-done | bytes 102416
  581.0 32.8 %all-reduce.1 = (f32[4]{0:T(128)S(1)}, f32[4]{0:T(128)S(1)}, f32[]{:T(128)}) all-reduce(f32[4]{0:T(128)S(1)} %pad_maximum_fusion.4, f32[4]{0:T(128)S(1)} %multiply_reduce_fusion, f32[]{:T(128)} %get-tuple-element.9), channel_id=1, replica_groups=mesh['region'=32,'grp'=16] {'grp'}, use_global_device_ids=true, to_apply=%region_8.9 | all-reduce | flops 9 | bytes 72 | tf_op jit(solution)/shard_map/psum | solution.py:147
  613.8 61.2 %all-reduce = (f32[4]{0:T(128)S(1)}, f32[4]{0:T(128)S(1)}, f32[]{:T(128)}) all-reduce(f32[4]{0:T(128)S(1)} %get-tuple-element.13, f32[4]{0:T(128)S(1)} %get-tuple-element.14, f32[]{:T(128)} %get-tuple-element.15), channel_id=1, replica_groups=mesh['region'=32,'grp'=16] {'region'}, use_global_device_ids=true, to_apply=%region_9.10 | all-reduce | flops 9 | bytes 72 | tf_op jit(solution)/shard_map/psum | solution.py:146
  676.3 99.9 %psum.104 = f32[]{:T(128)} all-reduce(f32[]{:T(128)} %get-tuple-element.7), channel_id=1, replica_groups=mesh['region'=32,'grp'=16] {'region','grp'}, use_global_device_ids=true, to_apply=%region_17.18 | all-reduce | flops 1 | bytes 8 | tf_op jit(solution)/shard_map/psum | solution.py:163
  778.9 96.3 %psum.105 = f32[]{:T(128)} all-reduce(f32[]{:T(128)} %fusion.95), channel_id=1, replica_groups=mesh['region'=32,'grp'=16] {'region','grp'}, use_global_device_ids=true, to_apply=%region_19.20 | all-reduce | flops 1 | bytes 8 | tf_op jit(solution)/shard_map/psum | solution.py:163
  877.9 95.3 %psum.106 = f32[]{:T(128)} all-reduce(f32[]{:T(128)} %get-tuple-element.20), channel_id=1, replica_groups=mesh['region'=32,'grp'=16] {'region','grp'}, use_global_device_ids=true, to_apply=%region_21.22 | all-reduce | flops 1 | bytes 8 | tf_op jit(solution)/shard_map/psum | solution.py:163
  976.4 96.4 %psum.107 = f32[]{:T(128)} all-reduce(f32[]{:T(128)} %fusion.106), channel_id=1, replica_groups=mesh['region'=32,'grp'=16] {'region','grp'}, use_global_device_ids=true, to_apply=%region_23.24 | all-reduce | flops 1 | bytes 8 | tf_op jit(solution)/shard_map/psum | solution.py:163
  1075.4 95.4 %psum.108 = f32[]{:T(128)} all-reduce(f32[]{:T(128)} %get-tuple-element.18), channel_id=1, replica_groups=mesh['region'=32,'grp'=16] {'region','grp'}, use_global_device_ids=true, to_apply=%region_25.26 | all-reduce | flops 1 | bytes 8 | tf_op jit(solution)/shard_map/psum | solution.py:170
  1172.2 96.3 %psum.109 = f32[]{:T(128)} all-reduce(f32[]{:T(128)} %fusion.99), channel_id=1, replica_groups=mesh['region'=32,'grp'=16] {'region','grp'}, use_global_device_ids=true, to_apply=%region_27.28 | all-reduce | flops 1 | bytes 8 | tf_op jit(solution)/shard_map/psum | solution.py:170
  1269.8 95.3 %psum.110 = f32[]{:T(128)} all-reduce(f32[]{:T(128)} %get-tuple-element.16), channel_id=1, replica_groups=mesh['region'=32,'grp'=16] {'region','grp'}, use_global_device_ids=true, to_apply=%region_29.30 | all-reduce | flops 1 | bytes 8 | tf_op jit(solution)/shard_map/psum | solution.py:170
  1366.5 96.3 %psum.111 = f32[]{:T(128)} all-reduce(f32[]{:T(128)} %multiply_reduce_fusion.1), channel_id=1, replica_groups=mesh['region'=32,'grp'=16] {'region','grp'}, use_global_device_ids=true, to_apply=%region_31.32 | all-reduce | flops 1 | bytes 8 | tf_op jit(solution)/shard_map/psum | solution.py:170
  (90 shorter events, 96.8 us)
Async XLA Ops:
  7.2 94.3 %all-gather.2.cloned.1.call-start = ((), (), s32[]{:S(2)}) async-start(), calls=%async_computation.5 | async-start | bytes 1740800 | tf_op jit(solution)/shard_map/all_gather | solution.py:73
  177.4 4.4 copy-start.7
  254.7 2.8 copy-start.5
  263.9 17.9 %all-to-all-start.2 = ((bf16[16,2,8192]{2,1,0:T(2,128)(2,1)}), bf16[16,2,8192]{2,1,0:T(2,128)(2,1)}, u32[]{:S(2)}, u32[]{:S(2)}) async-start(bf16[16,2,8192]{2,1,0:T(2,128)(2,1)} %reshape.165), calls=%async_computation.2 | async-start | bytes 1048576 | tf_op jit(solution)/shard_map/all_to_all | solution.py:110
  268.3 308.3 %reduce-scatter.4.cloned.1.call-start = ((), (), s32[]{:S(2)}) async-start(), calls=%async_computation.6 | async-start | bytes 1740800
  302.8 4.4 copy-start.6
  376.0 4.5 copy-start.8
  410.3 1.5 copy-start
  411.8 165.8 %copy-start.1 = (f32[3,2,40,640]{3,2,1,0:T(8,128)S(1)}, f32[3,2,40,640]{3,2,1,0:T(8,128)}, u32[]{:S(2)}) copy-start(f32[3,2,40,640]{3,2,1,0:T(8,128)} %param.12) | copy-start | bytes 1843204
  411.8 165.8 %copy-start.2 = (f32[2,40,640]{2,1,0:T(8,128)S(1)}, f32[2,40,640]{2,1,0:T(8,128)}, u32[]{:S(2)}) copy-start(f32[2,40,640]{2,1,0:T(8,128)} %param.7) | copy-start | bytes 614404
  411.8 165.8 %copy-start.4 = (f32[2,40,640]{2,1,0:T(8,128)S(1)}, f32[2,40,640]{2,1,0:T(8,128)}, u32[]{:S(2)}) copy-start(f32[2,40,640]{2,1,0:T(8,128)} %param.13) | copy-start | bytes 614404
  578.4 691.4 %copy-start.3 = (f32[2,40,640]{2,1,0:T(8,128)}, f32[2,40,640]{2,1,0:T(8,128)S(1)}, u32[]{:S(2)}) copy-start(f32[2,40,640]{2,1,0:T(8,128)S(1)} %get-tuple-element.23) | copy-start | bytes 614404
Sparse Core Ops, SparseCore 0:
  11.8 89.6 all-gather.1
  411.9 164.6 reduce-scatter.3
